TPU v7x, 32 devices: a whole 2x2x4 slice. The times are simulated.
32 devices in a mesh: fsdp: 4 (over x, core), ctx: 8 (over z, y).
Axes of the slice: x: 2, y: 2, z: 4, core: 2. Of those that a mesh axis runs over, the one named last changes fastest.
Arguments:
- tokens: bfloat16 [4, 2048, 1024], P('fsdp', 'ctx'), may hold values from -6 to 6
- out_grad: bfloat16 [4, 2048, 1024], P('fsdp', 'ctx'), may hold values from -6 to 6
- slot_block: int32 [4, 16], P('fsdp'), may hold values from 0 to 15, as said below
- w_attend: bfloat16 [1024, 3072], P('fsdp'), may hold values from -0.1875 to 0.1875
- w_mixing: bfloat16 [1024, 1024], P('fsdp'), may hold values from -1 to 1
- w_expand: bfloat16 [1024, 4096], P('fsdp'), may hold values from -0.1875 to 0.1875
- w_shrink: bfloat16 [4096, 1024], P('fsdp'), may hold values from -0.09375 to 0.09375
- w_norms: bfloat16 [4, 1024], P(None, 'fsdp'), may hold values from -1.2 to 1.4
- first_attend: float32 [1024, 3072], P('fsdp'), may hold values from -24 to 24
- first_mixing: float32 [1024, 1024], P('fsdp'), may hold values from -24 to 24
- first_expand: float32 [1024, 4096], P('fsdp'), may hold values from -24 to 24
- first_shrink: float32 [4096, 1024], P('fsdp'), may hold values from -24 to 24
- first_norms: float32 [4, 1024], P(None, 'fsdp'), may hold values from -24 to 24
- second_attend: float32 [1024, 3072], P('fsdp'), may hold values from 0.5 to 8
- second_mixing: float32 [1024, 1024], P('fsdp'), may hold values from 0.5 to 8
- second_expand: float32 [1024, 4096], P('fsdp'), may hold values from 0.5 to 8
- second_shrink: float32 [4096, 1024], P('fsdp'), may hold values from 0.5 to 8
- second_norms: float32 [4, 1024], P(None, 'fsdp'), may hold values from 0.5 to 8
Outputs:
- layer_out: bfloat16 [4, 2048, 1024], P('fsdp', 'ctx')
- tokens_grad: float32 [4, 2048, 1024], P('fsdp', 'ctx')
- grad_attend: float32 [1024, 3072], P('fsdp')
- update_attend: float32 [1024, 3072], P('fsdp')
- first_new_attend: float32 [1024, 3072], P('fsdp')
- second_new_attend: float32 [1024, 3072], P('fsdp')
- grad_mixing: float32 [1024, 1024], P('fsdp')
- update_mixing: float32 [1024, 1024], P('fsdp')
- first_new_mixing: float32 [1024, 1024], P('fsdp')
- second_new_mixing: float32 [1024, 1024], P('fsdp')
- grad_expand: float32 [1024, 4096], P('fsdp')
- update_expand: float32 [1024, 4096], P('fsdp')
- first_new_expand: float32 [1024, 4096], P('fsdp')
- second_new_expand: float32 [1024, 4096], P('fsdp')
- grad_shrink: float32 [4096, 1024], P('fsdp')
- update_shrink: float32 [4096, 1024], P('fsdp')
- first_new_shrink: float32 [4096, 1024], P('fsdp')
- second_new_shrink: float32 [4096, 1024], P('fsdp')
- grad_norms: float32 [4, 1024], P(None, 'fsdp')
- update_norms: float32 [4, 1024], P(None, 'fsdp')
- first_new_norms: float32 [4, 1024], P(None, 'fsdp')
- second_new_norms: float32 [4, 1024], P(None, 'fsdp')
Inputs may be any that keep to these rules, and one draw needn't show every extreme that they name: `slot_block`: in each row every block number appears once, and slots 2i and 2i+1 hold two blocks whose numbers add up to 15.
All inputs are finite; a program needn't handle non-finite values.
Results may differ from a plain program's by a relative error of at most 0.025.
Values may be sent and summed in bfloat16 or wider, within the bound.
A program may use at most 256 MiB of HBM per device.

v0:
```python
import math
import jax
import jax.numpy as jnp
from jax import lax
from jax.sharding import PartitionSpec as P

HD = 64
HGROUP = 2
STEP_COUNT = 10
EPS_NORM = 1e-05
NEG = -1e30
BETA_ONE = 0.9
BETA_TWO = 0.999
LEARN = 0.02
DECAY = 0.1
EPS_ADAM = 1e-08
CUBIC = 0.044715
ROOT_TWO_PI = math.sqrt(2.0 / math.pi)


def layer_norm(values, gain, shift):
    center = values - jnp.mean(values, axis=-1, keepdims=True)
    spread = jnp.mean(center * center, axis=-1, keepdims=True)
    return center * lax.rsqrt(spread + EPS_NORM) * gain + shift


def gelu(values):
    cube = values * values * values
    return 0.5 * values * (1.0 + jnp.tanh(ROOT_TWO_PI * (values + CUBIC * cube)))


def positions(slots, block):
    offsets = jnp.arange(block, dtype=jnp.int32)
    placed = slots[:, :, None] * block + offsets[None, None, :]
    return placed.reshape(slots.shape[0], slots.shape[1] * block)


def adam_step(weight, grad, first, second):
    first_new = BETA_ONE * first + (1.0 - BETA_ONE) * grad
    second_new = BETA_TWO * second + (1.0 - BETA_TWO) * grad * grad
    mean_hat = first_new / (1.0 - BETA_ONE**STEP_COUNT)
    square_hat = second_new / (1.0 - BETA_TWO**STEP_COUNT)
    update = -LEARN * (
        mean_hat / (jnp.sqrt(square_hat) + EPS_ADAM) + DECAY * weight.astype(jnp.float32)
    )
    return (update, first_new, second_new)


def shards(
    tokens,
    out_grad,
    slot_block,
    w_attend,
    w_mixing,
    w_expand,
    w_shrink,
    w_norms,
    first_attend,
    first_mixing,
    first_expand,
    first_shrink,
    first_norms,
    second_attend,
    second_mixing,
    second_expand,
    second_shrink,
    second_norms,
):
    whole_attend, whole_mixing, whole_expand, whole_shrink, whole_norms = (
        lax.all_gather(w_attend, "fsdp", axis=0, tiled=True),
        lax.all_gather(w_mixing, "fsdp", axis=0, tiled=True),
        lax.all_gather(w_expand, "fsdp", axis=0, tiled=True),
        lax.all_gather(w_shrink, "fsdp", axis=0, tiled=True),
        lax.all_gather(w_norms, "fsdp", axis=1, tiled=True),
    )
    seqs, local, width = tokens.shape
    block = local // 2
    length = slot_block.shape[1] * block
    total_rows = seqs * local
    heads = width // HD
    group_width = HGROUP * HD
    scale = 1.0 / math.sqrt(HD)
    norm_values = whole_norms.astype(jnp.float32)
    owned = lax.dynamic_slice_in_dim(slot_block, 2 * lax.axis_index("ctx"), 2, 1)
    query_place = positions(owned, block)
    key_place = positions(slot_block, block)
    allowed = key_place[:, None, None, :] <= query_place[:, None, :, None]
    start = tokens.reshape(total_rows, width).astype(jnp.float32)
    normed, norm_back = jax.vjp(layer_norm, start, norm_values[0], norm_values[1])
    normed_low = normed.astype(jnp.bfloat16)
    joint = jnp.dot(normed_low, whole_attend, preferred_element_type=jnp.float32).astype(
        jnp.bfloat16
    )
    query = joint[:, :width].reshape(seqs, local, width)
    keys_own = joint[:, width : 2 * width].reshape(seqs, local, width)
    values_own = joint[:, 2 * width :].reshape(seqs, local, width)
    keys, values = (
        lax.all_gather(keys_own, "ctx", axis=1, tiled=True),
        lax.all_gather(values_own, "ctx", axis=1, tiled=True),
    )

    def group_scores(index):
        offset = index * group_width
        query_group = lax.dynamic_slice_in_dim(query, offset, group_width, 2).reshape(
            seqs, local, HGROUP, HD
        )
        key_group = lax.dynamic_slice_in_dim(keys, offset, group_width, 2).reshape(
            seqs, length, HGROUP, HD
        )
        value_group = lax.dynamic_slice_in_dim(values, offset, group_width, 2).reshape(
            seqs, length, HGROUP, HD
        )
        raw = (
            jnp.einsum(
                "sqhd,skhd->shqk", query_group, key_group, preferred_element_type=jnp.float32
            )
            * scale
        )
        return (jnp.where(allowed, raw, NEG), query_group, key_group, value_group)

    def forward_group(index, state):
        mixed_buffer, totals_buffer = state
        masked, query_group, key_group, value_group = group_scores(index)
        top = jnp.max(masked, axis=-1, keepdims=True)
        total = top + jnp.log(jnp.sum(jnp.exp(masked - top), axis=-1, keepdims=True))
        probs = jnp.exp(masked - total).astype(jnp.bfloat16)
        result = jnp.einsum(
            "shqk,skhd->sqhd", probs, value_group, preferred_element_type=jnp.float32
        )
        result = result.reshape(seqs, local, group_width).astype(jnp.bfloat16)
        mixed_buffer = lax.dynamic_update_slice_in_dim(mixed_buffer, result, index * group_width, 2)
        totals_buffer = lax.dynamic_update_slice_in_dim(
            totals_buffer, total[..., 0], index * HGROUP, 1
        )
        return (mixed_buffer, totals_buffer)

    mixed, totals = lax.fori_loop(
        0,
        heads // HGROUP,
        forward_group,
        (
            jnp.zeros((seqs, local, width), jnp.bfloat16),
            jnp.zeros((seqs, heads, local), jnp.float32),
        ),
    )
    mixed_rows = mixed.reshape(total_rows, width)
    middle = start + jnp.dot(mixed_rows, whole_mixing, preferred_element_type=jnp.float32)
    normed_two, norm_two_back = jax.vjp(layer_norm, middle, norm_values[2], norm_values[3])
    normed_two_low = normed_two.astype(jnp.bfloat16)
    expanded = jnp.dot(normed_two_low, whole_expand, preferred_element_type=jnp.float32)
    activated, gelu_back = jax.vjp(gelu, expanded)
    activated_low = activated.astype(jnp.bfloat16)
    result_rows = middle + jnp.dot(activated_low, whole_shrink, preferred_element_type=jnp.float32)
    layer_out = result_rows.reshape(seqs, local, width).astype(jnp.bfloat16)
    incoming = out_grad.reshape(total_rows, width)
    grad_shrink = jnp.dot(activated_low.T, incoming, preferred_element_type=jnp.float32)
    grad_activated = jnp.dot(incoming, whole_shrink.T, preferred_element_type=jnp.float32).astype(
        jnp.bfloat16
    )
    grad_expanded = gelu_back(grad_activated.astype(jnp.float32))[0].astype(jnp.bfloat16)
    grad_expand = jnp.dot(normed_two_low.T, grad_expanded, preferred_element_type=jnp.float32)
    grad_normed_two = jnp.dot(grad_expanded, whole_expand.T, preferred_element_type=jnp.float32)
    grad_middle_norm, grad_gain_two, grad_shift_two = norm_two_back(grad_normed_two)
    grad_middle = incoming.astype(jnp.float32) + grad_middle_norm
    grad_branch = grad_middle.astype(jnp.bfloat16)
    grad_mixing = jnp.dot(mixed_rows.T, grad_branch, preferred_element_type=jnp.float32)
    grad_mixed = jnp.dot(grad_branch, whole_mixing.T, preferred_element_type=jnp.float32)
    grad_mixed = grad_mixed.astype(jnp.bfloat16).reshape(seqs, local, width)

    def backward_group(index, state):
        grad_query, grad_keys, grad_values = state
        offset = index * group_width
        masked, query_group, key_group, value_group = group_scores(index)
        total = lax.dynamic_slice_in_dim(totals, index * HGROUP, HGROUP, 1)
        probs = jnp.exp(masked - total[..., None])
        grad_group = lax.dynamic_slice_in_dim(grad_mixed, offset, group_width, 2).reshape(
            seqs, local, HGROUP, HD
        )
        grad_probs = jnp.einsum(
            "sqhd,skhd->shqk", grad_group, value_group, preferred_element_type=jnp.float32
        )
        grad_scores = probs * (grad_probs - jnp.sum(probs * grad_probs, axis=-1, keepdims=True))
        grad_scores = grad_scores.astype(jnp.bfloat16)
        part_query = (
            jnp.einsum(
                "shqk,skhd->sqhd", grad_scores, key_group, preferred_element_type=jnp.float32
            )
            * scale
        )
        part_keys = (
            jnp.einsum(
                "shqk,sqhd->skhd", grad_scores, query_group, preferred_element_type=jnp.float32
            )
            * scale
        )
        part_values = jnp.einsum(
            "shqk,sqhd->skhd",
            probs.astype(jnp.bfloat16),
            grad_group,
            preferred_element_type=jnp.float32,
        )
        grad_query = lax.dynamic_update_slice_in_dim(
            grad_query, part_query.reshape(seqs, local, group_width), offset, 2
        )
        grad_keys = lax.dynamic_update_slice_in_dim(
            grad_keys, part_keys.reshape(seqs, length, group_width), offset, 2
        )
        grad_values = lax.dynamic_update_slice_in_dim(
            grad_values, part_values.reshape(seqs, length, group_width), offset, 2
        )
        return (grad_query, grad_keys, grad_values)

    grad_query, grad_keys_all, grad_values_all = lax.fori_loop(
        0,
        heads // HGROUP,
        backward_group,
        (
            jnp.zeros((seqs, local, width), jnp.float32),
            jnp.zeros((seqs, length, width), jnp.float32),
            jnp.zeros((seqs, length, width), jnp.float32),
        ),
    )
    grad_keys, grad_values = (
        lax.psum_scatter(
            grad_keys_all.astype(jnp.bfloat16), "ctx", scatter_dimension=1, tiled=True
        ).astype(jnp.float32),
        lax.psum_scatter(
            grad_values_all.astype(jnp.bfloat16), "ctx", scatter_dimension=1, tiled=True
        ).astype(jnp.float32),
    )
    grad_joint = jnp.concatenate(
        [
            grad_query.astype(jnp.bfloat16),
            grad_keys.astype(jnp.bfloat16),
            grad_values.astype(jnp.bfloat16),
        ],
        axis=2,
    ).reshape(total_rows, 3 * width)
    grad_attend = jnp.dot(normed_low.T, grad_joint, preferred_element_type=jnp.float32)
    grad_normed = jnp.dot(grad_joint, whole_attend.T, preferred_element_type=jnp.float32)
    grad_start_norm, grad_gain_one, grad_shift_one = norm_back(grad_normed)
    tokens_grad = (grad_middle + grad_start_norm).reshape(seqs, local, width)
    grad_norms = jnp.stack([grad_gain_one, grad_shift_one, grad_gain_two, grad_shift_two])
    owned_attend, owned_mixing, owned_expand, owned_shrink, owned_norms = (
        lax.psum_scatter(
            grad_attend.astype(jnp.bfloat16), "fsdp", scatter_dimension=0, tiled=True
        ).astype(jnp.float32),
        lax.psum_scatter(
            grad_mixing.astype(jnp.bfloat16), "fsdp", scatter_dimension=0, tiled=True
        ).astype(jnp.float32),
        lax.psum_scatter(
            grad_expand.astype(jnp.bfloat16), "fsdp", scatter_dimension=0, tiled=True
        ).astype(jnp.float32),
        lax.psum_scatter(
            grad_shrink.astype(jnp.bfloat16), "fsdp", scatter_dimension=0, tiled=True
        ).astype(jnp.float32),
        lax.psum_scatter(
            grad_norms.astype(jnp.bfloat16), "fsdp", scatter_dimension=1, tiled=True
        ).astype(jnp.float32),
    )
    sum_attend, sum_mixing, sum_expand, sum_shrink, sum_norms = (
        lax.psum(owned_attend.astype(jnp.bfloat16), "ctx").astype(jnp.float32),
        lax.psum(owned_mixing.astype(jnp.bfloat16), "ctx").astype(jnp.float32),
        lax.psum(owned_expand.astype(jnp.bfloat16), "ctx").astype(jnp.float32),
        lax.psum(owned_shrink.astype(jnp.bfloat16), "ctx").astype(jnp.float32),
        lax.psum(owned_norms.astype(jnp.bfloat16), "ctx").astype(jnp.float32),
    )
    update_attend, first_new_attend, second_new_attend = adam_step(
        w_attend, sum_attend, first_attend, second_attend
    )
    update_mixing, first_new_mixing, second_new_mixing = adam_step(
        w_mixing, sum_mixing, first_mixing, second_mixing
    )
    update_expand, first_new_expand, second_new_expand = adam_step(
        w_expand, sum_expand, first_expand, second_expand
    )
    update_shrink, first_new_shrink, second_new_shrink = adam_step(
        w_shrink, sum_shrink, first_shrink, second_shrink
    )
    update_norms, first_new_norms, second_new_norms = adam_step(
        w_norms, sum_norms, first_norms, second_norms
    )
    return (
        layer_out,
        tokens_grad,
        sum_attend,
        update_attend,
        first_new_attend,
        second_new_attend,
        sum_mixing,
        update_mixing,
        first_new_mixing,
        second_new_mixing,
        sum_expand,
        update_expand,
        first_new_expand,
        second_new_expand,
        sum_shrink,
        update_shrink,
        first_new_shrink,
        second_new_shrink,
        sum_norms,
        update_norms,
        first_new_norms,
        second_new_norms,
    )


def solution(mesh):
    return jax.shard_map(
        shards,
        mesh=mesh,
        in_specs=(
            P("fsdp", "ctx", None),
            P("fsdp", "ctx", None),
            P("fsdp", None),
            P("fsdp", None),
            P("fsdp", None),
            P("fsdp", None),
            P("fsdp", None),
            P(None, "fsdp"),
            P("fsdp", None),
            P("fsdp", None),
            P("fsdp", None),
            P("fsdp", None),
            P(None, "fsdp"),
            P("fsdp", None),
            P("fsdp", None),
            P("fsdp", None),
            P("fsdp", None),
            P(None, "fsdp"),
        ),
        out_specs=(
            P("fsdp", "ctx", None),
            P("fsdp", "ctx", None),
            P("fsdp", None),
            P("fsdp", None),
            P("fsdp", None),
            P("fsdp", None),
            P("fsdp", None),
            P("fsdp", None),
            P("fsdp", None),
            P("fsdp", None),
            P("fsdp", None),
            P("fsdp", None),
            P("fsdp", None),
            P("fsdp", None),
            P("fsdp", None),
            P("fsdp", None),
            P("fsdp", None),
            P("fsdp", None),
            P(None, "fsdp"),
            P(None, "fsdp"),
            P(None, "fsdp"),
            P(None, "fsdp"),
        ),
        check_vma=False,
    )
```

profile of v0, /device:TPU:0, one launch (start us, length us, event | category | flops | bytes accessed | tf_op | source)
XLA Modules:
  0.0 1199.6 jit_solution(6608566212357250092)
XLA Ops:
  8.0 6.3 all_gather.21
  16.8 41.9 %all-gather.9.cloned.1.call-done = bf16[1024,3072]{1,0:T(8,128)(2,1)} async-done(((bf16[256,3072]{1,0:T(8,128)(2,1)}), bf16[1024,3072]{1,0:T(8,128)(2,1)}) %all-gather.9.cloned.1.call-update) | async-done | bytes 6291472 | tf_op jit(solution)/shard_map/all_gather | solution.py:70
  58.7 4.9 convolution_convert_fusion.4
  67.8 70.6 %all-gather.17.cloned.1.call-done = bf16[2048,1024]{1,0:T(8,128)(2,1)} async-done(((bf16[256,1024]{1,0:T(8,128)(2,1)}), bf16[2048,1024]{1,0:T(8,128)(2,1)}) %all-gather.17.cloned.1.call-update) | async-done | bytes 4194320 | tf_op jit(solution)/shard_map/all_gather | solution.py:99
  138.4 6.4 copy.47
  144.8 68.0 %all-gather.19.cloned.1.call-done = bf16[2048,1024]{1,0:T(8,128)(2,1)} async-done(((bf16[256,1024]{1,0:T(8,128)(2,1)}), bf16[2048,1024]{1,0:T(8,128)(2,1)}) %all-gather.19.cloned.1.call-update) | async-done | bytes 4194320 | tf_op jit(solution)/shard_map/all_gather | solution.py:98
  212.8 6.4 copy.49
  219.3 74.3 %while.34 = (s32[]{:T(128)}, bf16[1,256,1024]{1,2,0:T(8,128)(2,1)S(1)}, f32[1,16,256]{2,1,0:T(8,128)S(1)}, bf16[1,2048,1024]{1,2,0:T(8,128)(2,1)}, bf16[1,256,10...) while((s32[]{:T(128)}, ...), condition=%wide.region_5.6_spmd.clone, body=%wide.region_2.5_spmd.clone.sunk | while | flops 276332032 | bytes 33973524 | solution.py:137
  221.0 3.0 fusion.120
  224.1 3.1 exponential_reduce_fusion.2
  230.2 3.0 fusion.120
  233.2 3.1 exponential_reduce_fusion.2
  239.3 3.0 fusion.120
  242.3 3.6 exponential_reduce_fusion.2
  249.6 3.0 fusion.120
  258.8 3.0 fusion.120
  267.9 3.0 fusion.120
  270.9 3.1 exponential_reduce_fusion.2
  297.1 7.9 fusion.64
  305.0 49.5 %all-gather.15.cloned.1.call-done = bf16[4096,1024]{1,0:T(8,128)(2,1)} async-done(((bf16[1024,1024]{1,0:T(8,128)(2,1)}), bf16[4096,1024]{1,0:T(8,128)(2,1)}) %all-gather.15.cloned.1.call-update) | async-done | bytes 8388624 | tf_op jit(solution)/shard_map/all_gather | solution.py:73
  354.6 8.7 fusion.17
  375.0 120.1 %while.35 = (s32[]{:T(128)}, bf16[1,256,1024]{1,2,0:T(8,128)(2,1)}, bf16[1,2048,1024]{1,2,0:T(8,128)(2,1)}, bf16[1,2048,1024]{1,2,0:T(8,128)(2,1)}, bf16[1,2048,...) while((s32[]{:T(128)}, bf16[1,256,1024]{1,2,0:T(8,128)(2,1)}, ...), condition=%wide.region_12.13_spmd.clone, body=%wide.region_10.0_spmd.clone.sunk | while | flops 681639424 | bytes 56970552 | solution.py:213
  382.1 4.0 multiply_reduce_fusion.5
  397.2 4.0 multiply_reduce_fusion.5
  412.2 4.0 multiply_reduce_fusion.5
  427.2 4.0 multiply_reduce_fusion.5
  442.2 4.0 multiply_reduce_fusion.5
  457.2 4.0 multiply_reduce_fusion.5
  472.2 4.0 multiply_reduce_fusion.5
  487.2 4.0 multiply_reduce_fusion.5
  496.2 3.1 convolution_convert_fusion.5
  499.5 7.3 convolution_convert_fusion.1
  507.9 8.5 convolution_convert_fusion
  516.4 67.2 %reduce-scatter.12.cloned.1.call-done = bf16[1,256,1024]{1,2,0:T(8,128)(2,1)} async-done(((bf16[1,2048,1024]{1,2,0:T(8,128)(2,1)}), bf16[1,256,1024]{1,2,0:T(8,128)(2,1)}) %reduce-scatter.12.cloned.1.call-update) | async-done | bytes 524304 | tf_op jit(solution)/shard_map/reduce_scatter | solution.py:227
  583.6 92.7 %reduce-scatter.10.cloned.1.call-done = bf16[1,256,1024]{1,2,0:T(8,128)(2,1)} async-done(((bf16[1,2048,1024]{1,2,0:T(8,128)(2,1)}), bf16[1,256,1024]{1,2,0:T(8,128)(2,1)}) %reduce-scatter.10.cloned.1.call-update) | async-done | bytes 524304 | tf_op jit(solution)/shard_map/reduce_scatter | solution.py:224
  676.4 6.0 convolution_convert_fusion.2
  682.5 5.4 fusion.35
  690.7 20.0 %reduce-scatter.16.cloned.1.call-done = bf16[256,1024]{1,0:T(8,128)(2,1)} async-done(((bf16[1024,1024]{1,0:T(8,128)(2,1)}), bf16[256,1024]{1,0:T(8,128)(2,1)}) %reduce-scatter.16.cloned.1.call-update) | async-done | bytes 524304 | tf_op jit(solution)/shard_map/reduce_scatter | solution.py:248
  710.7 74.4 %reduce-scatter.18.cloned.1.call-done = bf16[256,4096]{1,0:T(8,128)(2,1)} async-done(((bf16[1024,4096]{1,0:T(8,128)(2,1)}), bf16[256,4096]{1,0:T(8,128)(2,1)}) %reduce-scatter.18.cloned.1.call-update) | async-done | bytes 2097168 | tf_op jit(solution)/shard_map/reduce_scatter | solution.py:251
  785.0 74.3 %reduce-scatter.20.cloned.1.call-done = bf16[1024,1024]{1,0:T(8,128)(2,1)} async-done(((bf16[4096,1024]{1,0:T(8,128)(2,1)}), bf16[1024,1024]{1,0:T(8,128)(2,1)}) %reduce-scatter.20.cloned.1.call-update) | async-done | bytes 2097168 | tf_op jit(solution)/shard_map/reduce_scatter | solution.py:254
  859.4 60.9 %reduce-scatter.14.cloned.1.call-done = bf16[256,3072]{1,0:T(8,128)(2,1)} async-done(((bf16[1024,3072]{1,0:T(8,128)(2,1)}), bf16[256,3072]{1,0:T(8,128)(2,1)}) %reduce-scatter.14.cloned.1.call-update) | async-done | bytes 1572880 | tf_op jit(solution)/shard_map/reduce_scatter | solution.py:245
  920.4 8.3 fusion.28
  930.2 13.3 %reduce-scatter.22.cloned.1.call-done = bf16[256,4]{1,0:T(8,128)(2,1)} async-done(((bf16[1024,4]{1,0:T(8,128)(2,1)}), bf16[256,4]{1,0:T(8,128)(2,1)}) %reduce-scatter.22.cloned.1.call-update) | async-done | bytes 2064
  944.4 21.8 %psum.39 = bf16[4,256]{1,0:T(4,128)(2,1)S(1)} all-reduce(bf16[4,256]{1,0:T(4,128)(2,1)S(1)} %copy.55), channel_id=1, replica_groups=mesh['fsdp'=4,'ctx'=8] {'ctx'}, use_global_device_ids=true, to_apply=%region_30.31 | all-reduce | flops 1024 | bytes 4096 | tf_op jit(solution)/shard_map/psum | solution.py:266
  966.8 196.3 %all-reduce.3.cloned.1.call-done = (bf16[256,3072]{1,0:T(8,128)(2,1)}, bf16[256,1024]{1,0:T(8,128)(2,1)}, bf16[256,4096]{1,0:T(8,128)(2,1)}, bf16[1024,1024]{1,0:T(8,128)(2,1)}) async-done(((bf16[256,3072]{1,0:T(8,128)(2,1)}, bf16[256,1024]{1,0:T(8,128)(2,1)}, bf16[256,4096]{1,0:T(8,128)(2,1)}, bf16[1024,1024]{1,0:T(8,128)(2,1)}), (bf16[256,3072]{1,0:T(8,128)(2,1)}, bf16[256,1024]{1,0:T(8,128)(2,1)}, ...) | async-done | bytes 6291472 | tf_op jit(solution)/shard_map/psum | solution.py:262
  1163.2 8.7 add_multiply_fusion.2
  1176.2 9.8 add_multiply_fusion.1
  1186.1 6.8 add_multiply_fusion
  (333 shorter events, 165.2 us)
Async XLA Ops:
  7.2 51.5 %all-gather.9.cloned.1.call-start = ((), (), s32[]{:S(2)}) async-start(), calls=%async_computation.7 | async-start | bytes 7864320 | tf_op jit(solution)/shard_map/all_gather | solution.py:70
  7.9 130.4 %all-gather.17.cloned.1.call-start = ((), (), s32[]{:S(2)}) async-start(), calls=%async_computation.17 | async-start | bytes 4718592 | tf_op jit(solution)/shard_map/all_gather | solution.py:99
  16.8 46.8 %copy-start.27 = (f32[256]{0:T(256)}, f32[256]{0:T(256)S(1)}, u32[]{:S(2)}) copy-start(f32[256]{0:T(256)S(1)} %fusion.34) | copy-start | bytes 3076
  63.6 3.7 copy-start.33
  64.7 148.0 %all-gather.19.cloned.1.call-start = ((), (), s32[]{:S(2)}) async-start(), calls=%async_computation.18 | async-start | bytes 4718592 | tf_op jit(solution)/shard_map/all_gather | solution.py:98
  65.5 228.1 %all-gather.11.cloned.1.call-start = ((), (), s32[]{:S(2)}) async-start(), calls=%async_computation.8 | async-start | bytes 2621440 | tf_op jit(solution)/shard_map/all_gather | solution.py:71
  66.1 231.0 %all-gather.13.cloned.1.call-start = ((), (), s32[]{:S(2)}) async-start(), calls=%async_computation.9 | async-start | bytes 10485760 | tf_op jit(solution)/shard_map/all_gather | solution.py:72
  66.6 287.9 %all-gather.15.cloned.1.call-start = ((), (), s32[]{:S(2)}) async-start(), calls=%async_computation.10 | async-start | bytes 10485760 | tf_op jit(solution)/shard_map/all_gather | solution.py:73
  67.2 516.4 %reduce-scatter.12.cloned.1.call-start = ((), (), s32[]{:S(2)}) async-start(), calls=%async_computation.12 | async-start | bytes 4718592 | tf_op jit(solution)/shard_map/reduce_scatter | solution.py:227
  219.2 75.1 %copy-start.2 = (bf16[1,256,1024]{2,1,0:T(8,128)(2,1)S(1)}, bf16[1,256,1024]{2,1,0:T(8,128)(2,1)}, u32[]{:S(2)}) copy-start(bf16[1,256,1024]{2,1,0:T(8,128)(2,1)} %param.22) | copy-start | bytes 1572868
  242.3 4.7 copy-start
  293.6 11.5 copy-start.6
  297.1 57.5 %copy-start.19 = (bf16[1,256,1024]{2,1,0:T(8,128)(2,1)S(1)}, bf16[1,256,1024]{2,1,0:T(8,128)(2,1)}, u32[]{:S(2)}) copy-start(bf16[1,256,1024]{2,1,0:T(8,128)(2,1)} %param.23) | copy-start | bytes 1572868
  354.6 8.7 copy-start.32
  367.6 7.4 copy-start.22
  382.1 4.0 copy-start.1
  397.1 4.0 copy-start.1
  412.2 4.0 copy-start.1
  427.2 4.0 copy-start.1
  442.2 4.0 copy-start.1
  457.2 4.0 copy-start.1
  472.2 4.0 copy-start.1
  487.2 4.0 copy-start.1
  495.2 181.2 %reduce-scatter.10.cloned.1.call-start = ((), (), s32[]{:S(2)}) async-start(), calls=%async_computation.11 | async-start | bytes 4718592 | tf_op jit(solution)/shard_map/reduce_scatter | solution.py:224
  495.9 214.7 %reduce-scatter.16.cloned.1.call-start = ((), (), s32[]{:S(2)}) async-start(), calls=%async_computation.14 | async-start | bytes 2621440 | tf_op jit(solution)/shard_map/reduce_scatter | solution.py:248
  499.3 285.8 %reduce-scatter.18.cloned.1.call-start = ((), (), s32[]{:S(2)}) async-start(), calls=%async_computation.15 | async-start | bytes 10485760 | tf_op jit(solution)/shard_map/reduce_scatter | solution.py:251
  506.9 352.5 %reduce-scatter.20.cloned.1.call-start = ((), (), s32[]{:S(2)}) async-start(), calls=%async_computation.16 | async-start | bytes 10485760 | tf_op jit(solution)/shard_map/reduce_scatter | solution.py:254
  516.4 160.0 %copy-start.26 = (bf16[1,256,1024]{1,2,0:T(8,128)(2,1)S(1)}, bf16[1,256,1024]{1,2,0:T(8,128)(2,1)}, u32[]{:S(2)}) copy-start(bf16[1,256,1024]{1,2,0:T(8,128)(2,1)} %get-tuple-element.320) | copy-start | bytes 1572868
  516.4 403.9 %reduce-scatter.14.cloned.1.call-start = ((), (), s32[]{:S(2)}) async-start(), calls=%async_computation.13 | async-start | bytes 7864320 | tf_op jit(solution)/shard_map/reduce_scatter | solution.py:245
  682.4 261.1 %reduce-scatter.22.cloned.1.call-start = ((), (), s32[]{:S(2)}) async-start(), calls=%async_computation.19 | async-start | bytes 327680
  682.5 5.5 copy-start.28
  690.4 472.7 %all-reduce.3.cloned.1.call-start = ((), (), s32[]{:S(2)}) async-start(), calls=%async_computation.20 | async-start | bytes 12582912 | tf_op jit(solution)/shard_map/psum | solution.py:262
  920.3 8.3 copy-start.13
  920.3 8.3 copy-start.21
  928.6 37.6 %copy-start.29 = (bf16[4,256]{1,0:T(4,128)(2,1)S(1)}, bf16[4,256]{1,0:T(4,128)(2,1)}, u32[]{:S(2)}) copy-start(bf16[4,256]{1,0:T(4,128)(2,1)} %param.29) | copy-start | bytes 6148
  928.7 37.6 %copy-start.30 = (f32[4,256]{1,0:T(4,128)S(1)}, f32[4,256]{1,0:T(4,128)}, u32[]{:S(2)}) copy-start(f32[4,256]{1,0:T(4,128)} %param.34) | copy-start | bytes 12292
  928.7 37.6 %copy-start.31 = (f32[4,256]{1,0:T(4,128)S(1)}, f32[4,256]{1,0:T(4,128)}, u32[]{:S(2)}) copy-start(f32[4,256]{1,0:T(4,128)} %param.39) | copy-start | bytes 12292
  928.7 234.5 %copy-start.5 = (bf16[256,3072]{1,0:T(8,128)(2,1)S(1)}, bf16[256,3072]{1,0:T(8,128)(2,1)}, u32[]{:S(2)}) copy-start(bf16[256,3072]{1,0:T(8,128)(2,1)} %param.25) | copy-start | bytes 4718596
  1163.1 8.7 copy-start.16
  1163.1 8.7 copy-start.23
  1163.1 8.7 copy-start.24
  1163.2 8.7 copy-start.25
  1163.2 11.2 copy-start.9
  1171.8 4.4 copy-start.8
  1176.2 9.9 copy-start.4
  1176.2 9.9 copy-start.10
  1176.2 9.9 copy-start.11
  1176.2 9.9 copy-start.15
  (14 other events, 35.1 us)
Sparse Core Ops, SparseCore 0:
  9.6 49.0 all-gather.8
  64.9 73.4 all-gather.16
  141.1 71.6 all-gather.18
  214.2 20.8 all-gather.10
  236.5 58.2 all-gather.12
  296.2 58.3 all-gather.14
  495.3 88.2 reduce-scatter.11
  588.3 88.0 reduce-scatter.9
  679.5 31.1 reduce-scatter.15
  713.3 71.7 reduce-scatter.17
  787.6 71.7 reduce-scatter.19
  861.9 58.3 reduce-scatter.13
  923.3 20.0 reduce-scatter.21
  948.4 214.6 all-reduce.2
where the time goes:
time: 1210 us; the launch traced here: 1200 us
  waiting for transfers between devices  833 us (69%)
  matrix products  166 us (14%)
  local copies, waits for them, and re-layouts  87.7 us (7%)
  other arithmetic  68.2 us (6%)
  blocking collectives  28.1 us (2%)
  between operations  14.6 us (1%)
    psum x1, waiting for transfers between devices, shards(): lax.psum(owned_attend.astype(jnp.bfloat16), 'ctx').astype(jnp.float32)  196 us
    reduce_scatter x1, waiting for transfers between devices, shards(): lax.psum_scatter(grad_keys_all.astype(jnp.bfloat16), 'ctx', scatter_dimen...  92.7 us
    reduce_scatter x1, waiting for transfers between devices, shards(): lax.psum_scatter(grad_expand.astype(jnp.bfloat16), 'fsdp', scatter_dimens...  74.4 us
    reduce_scatter x1, waiting for transfers between devices, shards(): lax.psum_scatter(grad_shrink.astype(jnp.bfloat16), 'fsdp', scatter_dimens...  74.3 us
    all_gather x1, waiting for transfers between devices, shards(): lax.all_gather(values_own, 'ctx', axis=1, tiled=True)  70.6 us
    all_gather x1, waiting for transfers between devices, shards(): lax.all_gather(keys_own, 'ctx', axis=1, tiled=True)  68 us
    reduce_scatter x1, waiting for transfers between devices, shards(): lax.psum_scatter(grad_values_all.astype(jnp.bfloat16), 'ctx', scatter_dim...  67.2 us
    reduce_scatter x1, waiting for transfers between devices, shards(): lax.psum_scatter(grad_attend.astype(jnp.bfloat16), 'fsdp', scatter_dimens...  60.9 us
  transfers between devices with their start and end apart: 14, of which 12 were waited for; matrix products, arithmetic and copies ran while one was open for 12% of the time, Pallas kernels for 0%

commit v1 on v0

--- a/solution.py
+++ b/solution.py
@@ -16,6 +16,19 @@
 EPS_ADAM = 1e-08
 CUBIC = 0.044715
 ROOT_TWO_PI = math.sqrt(2.0 / math.pi)
+
+
+def gather_around(x, axis, dim):
+    ways = lax.axis_size(axis)
+    up = [(d, (d + 1) % ways) for d in range(ways)]
+    down = [(d, (d - 1) % ways) for d in range(ways)]
+    earlier, later = ([x], [x])
+    for _ in range(ways // 2):
+        earlier.append(lax.ppermute(earlier[-1], axis, up))
+    for _ in range((ways - 1) // 2):
+        later.append(lax.ppermute(later[-1], axis, down))
+    line = jnp.concatenate([*earlier[::-1], *later[1:]], axis=dim)
+    return jnp.roll(line, (lax.axis_index(axis) - ways // 2) * x.shape[dim], axis=dim)
 
 
 def layer_norm(values, gain, shift):
@@ -70,7 +83,7 @@
         lax.all_gather(w_attend, "fsdp", axis=0, tiled=True),
         lax.all_gather(w_mixing, "fsdp", axis=0, tiled=True),
         lax.all_gather(w_expand, "fsdp", axis=0, tiled=True),
-        lax.all_gather(w_shrink, "fsdp", axis=0, tiled=True),
+        gather_around(w_shrink, "fsdp", 0),
         lax.all_gather(w_norms, "fsdp", axis=1, tiled=True),
     )
     seqs, local, width = tokens.shape

time: 1210 us -> 1150 us (0.950)
  waiting for transfers between devices: 833 us -> 763 us
  local copies, waits for them, and re-layouts: 87.7 us -> 105 us
    all_gather x1, waiting for transfers between devices: 70.6 us -> 0.02 us  [shards(): lax.all_gather(values_own, 'ctx', axis=1, tiled=True)]
    ppermute x0 -> x3, waiting for transfers between devices: none -> 70.6 us  [the longest x2 70.6 us: gather_around(): earlier.append(lax.ppermute(earlier[-1], axis, up))]
    all_gather x1 -> x0, waiting for transfers between devices: 49.5 us -> none  [shards(): lax.all_gather(w_shrink, 'fsdp', axis=0, tiled=True)]
    all_gather x1, waiting for transfers between devices: 68 us -> 50.1 us  [shards(): lax.all_gather(keys_own, 'ctx', axis=1, tiled=True)]
    unnamed x69 -> x84, local copies, waits for them, and re-layouts: 20.7 us -> 35.8 us
  transfers between devices with their start and end apart: 14 -> 16, of which waited for: 12 -> 12; matrix products, arithmetic and copies ran while one was open for 12% -> 12% of each run, Pallas kernels for 0% -> 0%
where the time goes in v1:
time: 1150 us
  waiting for transfers between devices  763 us (66%)
  matrix products  165 us (14%)
  local copies, waits for them, and re-layouts  105 us (9%)
  other arithmetic  68.2 us (6%)
  blocking collectives  28.1 us (2%)
  between operations  14.8 us (1%)
    psum x1, waiting for transfers between devices, shards(): lax.psum(owned_attend.astype(jnp.bfloat16), 'ctx').astype(jnp.float32)  196 us
    reduce_scatter x1, waiting for transfers between devices, shards(): lax.psum_scatter(grad_keys_all.astype(jnp.bfloat16), 'ctx', scatter_dimen...  92.8 us
    reduce_scatter x1, waiting for transfers between devices, shards(): lax.psum_scatter(grad_expand.astype(jnp.bfloat16), 'fsdp', scatter_dimens...  74.5 us
    reduce_scatter x1, waiting for transfers between devices, shards(): lax.psum_scatter(grad_shrink.astype(jnp.bfloat16), 'fsdp', scatter_dimens...  74.2 us
    ppermute x2, waiting for transfers between devices, gather_around(): earlier.append(lax.ppermute(earlier[-1], axis, up))  70.6 us
    reduce_scatter x1, waiting for transfers between devices, shards(): lax.psum_scatter(grad_values_all.astype(jnp.bfloat16), 'ctx', scatter_dim...  65.4 us
    reduce_scatter x1, waiting for transfers between devices, shards(): lax.psum_scatter(grad_attend.astype(jnp.bfloat16), 'fsdp', scatter_dimens...  61.1 us
    dot_general x16, matrix products, group_scores(): jnp.einsum('sqhd,skhd->shqk', query_group, key_group, preferred_element_t...  56.6 us
  transfers between devices with their start and end apart: 16, of which 12 were waited for; matrix products, arithmetic and copies ran while one was open for 12% of the time, Pallas kernels for 0%

profile of v1, /device:TPU:0, one launch (start us, length us, event | category | flops | bytes accessed | tf_op | source)
XLA Modules:
  0.0 1147.5 jit_solution(10896209411157313139)
XLA Ops:
  8.0 6.3 all_gather.18
  16.8 41.9 %all-gather.8.cloned.1.call-done = bf16[1024,3072]{1,0:T(8,128)(2,1)} async-done(((bf16[256,3072]{1,0:T(8,128)(2,1)}), bf16[1024,3072]{1,0:T(8,128)(2,1)}) %all-gather.8.cloned.1.call-update) | async-done | bytes 6291472 | tf_op jit(solution)/shard_map/all_gather | solution.py:83
  58.7 4.9 convolution_convert_fusion.3
  66.1 25.0 %collective-permute-done = bf16[1024,1024]{1,0:T(8,128)(2,1)} collective-permute-done((bf16[1024,1024]{1,0:T(8,128)(2,1)S(1)}, bf16[1024,1024]{1,0:T(8,128)(2,1)}, u32[]{:S(2)}, u32[]{:S(2)}) %collective-permute-start) | collective-permute-done | bytes 2097184 | tf_op jit(solution)/shard_map/ppermute | solution.py:27
  93.6 45.5 %collective-permute-done.1 = bf16[1024,1024]{1,0:T(8,128)(2,1)} collective-permute-done((bf16[1024,1024]{1,0:T(8,128)(2,1)}, bf16[1024,1024]{1,0:T(8,128)(2,1)}, u32[]{:S(2)}, u32[]{:S(2)}) %collective-permute-start.1) | collective-permute-done | bytes 2097184 | tf_op jit(solution)/shard_map/ppermute | solution.py:27
  150.2 5.7 copy-done.28
  156.2 6.5 copy.48
  162.6 50.1 %all-gather.16.cloned.1.call-done = bf16[2048,1024]{1,0:T(8,128)(2,1)} async-done(((bf16[256,1024]{1,0:T(8,128)(2,1)}), bf16[2048,1024]{1,0:T(8,128)(2,1)}) %all-gather.16.cloned.1.call-update) | async-done | bytes 4194320 | tf_op jit(solution)/shard_map/all_gather | solution.py:111
  212.8 6.4 copy.50
  219.3 74.3 %while.34 = (s32[]{:T(128)}, bf16[1,256,1024]{1,2,0:T(8,128)(2,1)S(1)}, f32[1,16,256]{2,1,0:T(8,128)S(1)}, bf16[1,2048,1024]{1,2,0:T(8,128)(2,1)}, bf16[1,256,10...) while((s32[]{:T(128)}, ...), condition=%wide.region_5.6_spmd.clone, body=%wide.region_2.5_spmd.clone.sunk | while | flops 276332032 | bytes 33973524 | solution.py:150
  221.0 3.0 fusion.139
  224.1 3.1 exponential_reduce_fusion.2
  230.2 3.0 fusion.139
  233.2 3.1 exponential_reduce_fusion.2
  242.3 3.6 exponential_reduce_fusion.2
  267.9 3.0 fusion.139
  270.9 3.1 exponential_reduce_fusion.2
  277.0 3.0 fusion.139
  286.2 3.0 fusion.139
  297.1 6.0 fusion.85
  303.1 9.5 fusion.27
  324.4 120.1 %while.35 = (s32[]{:T(128)}, bf16[1,256,1024]{1,2,0:T(8,128)(2,1)}, bf16[1,2048,1024]{1,2,0:T(8,128)(2,1)}, bf16[1,2048,1024]{1,2,0:T(8,128)(2,1)}, bf16[1,2048,...) while((s32[]{:T(128)}, bf16[1,256,1024]{1,2,0:T(8,128)(2,1)}, ...), condition=%wide.region_12.13_spmd.clone, body=%wide.region_10.12_spmd.clone.sunk | while | flops 681639424 | bytes 56970552 | solution.py:226
  331.5 4.0 multiply_reduce_fusion.5
  346.5 4.0 multiply_reduce_fusion.5
  361.5 4.0 multiply_reduce_fusion.5
  376.6 4.0 multiply_reduce_fusion.5
  391.6 4.0 multiply_reduce_fusion.5
  406.6 4.0 multiply_reduce_fusion.5
  421.6 4.0 multiply_reduce_fusion.5
  436.6 4.0 multiply_reduce_fusion.5
  445.6 3.1 convolution_convert_fusion.4
  448.9 7.6 convolution_convert_fusion.1
  457.5 8.5 convolution_convert_fusion
  466.1 65.4 %reduce-scatter.12.cloned.1.call-done = bf16[1,256,1024]{1,2,0:T(8,128)(2,1)} async-done(((bf16[1,2048,1024]{1,2,0:T(8,128)(2,1)}), bf16[1,256,1024]{1,2,0:T(8,128)(2,1)}) %reduce-scatter.12.cloned.1.call-update) | async-done | bytes 524304 | tf_op jit(solution)/shard_map/reduce_scatter | solution.py:240
  531.5 92.8 %reduce-scatter.10.cloned.1.call-done = bf16[1,256,1024]{1,2,0:T(8,128)(2,1)} async-done(((bf16[1,2048,1024]{1,2,0:T(8,128)(2,1)}), bf16[1,256,1024]{1,2,0:T(8,128)(2,1)}) %reduce-scatter.10.cloned.1.call-update) | async-done | bytes 524304 | tf_op jit(solution)/shard_map/reduce_scatter | solution.py:237
  624.3 5.8 convolution_convert_fusion.2
  630.2 5.4 fusion.54
  638.5 20.1 %reduce-scatter.16.cloned.1.call-done = bf16[256,1024]{1,0:T(8,128)(2,1)} async-done(((bf16[1024,1024]{1,0:T(8,128)(2,1)}), bf16[256,1024]{1,0:T(8,128)(2,1)}) %reduce-scatter.16.cloned.1.call-update) | async-done | bytes 524304 | tf_op jit(solution)/shard_map/reduce_scatter | solution.py:261
  658.6 74.5 %reduce-scatter.18.cloned.1.call-done = bf16[256,4096]{1,0:T(8,128)(2,1)} async-done(((bf16[1024,4096]{1,0:T(8,128)(2,1)}), bf16[256,4096]{1,0:T(8,128)(2,1)}) %reduce-scatter.18.cloned.1.call-update) | async-done | bytes 2097168 | tf_op jit(solution)/shard_map/reduce_scatter | solution.py:264
  733.1 74.2 %reduce-scatter.20.cloned.1.call-done = bf16[1024,1024]{1,0:T(8,128)(2,1)} async-done(((bf16[4096,1024]{1,0:T(8,128)(2,1)}), bf16[1024,1024]{1,0:T(8,128)(2,1)}) %reduce-scatter.20.cloned.1.call-update) | async-done | bytes 2097168 | tf_op jit(solution)/shard_map/reduce_scatter | solution.py:267
  807.3 61.1 %reduce-scatter.14.cloned.1.call-done = bf16[256,3072]{1,0:T(8,128)(2,1)} async-done(((bf16[1024,3072]{1,0:T(8,128)(2,1)}), bf16[256,3072]{1,0:T(8,128)(2,1)}) %reduce-scatter.14.cloned.1.call-update) | async-done | bytes 1572880 | tf_op jit(solution)/shard_map/reduce_scatter | solution.py:258
  868.4 8.3 fusion.44
  878.2 13.1 %reduce-scatter.22.cloned.1.call-done = bf16[256,4]{1,0:T(8,128)(2,1)} async-done(((bf16[1024,4]{1,0:T(8,128)(2,1)}), bf16[256,4]{1,0:T(8,128)(2,1)}) %reduce-scatter.22.cloned.1.call-update) | async-done | bytes 2064
  892.3 21.8 %psum.39 = bf16[4,256]{1,0:T(4,128)(2,1)S(1)} all-reduce(bf16[4,256]{1,0:T(4,128)(2,1)S(1)} %copy.58), channel_id=1, replica_groups=mesh['fsdp'=4,'ctx'=8] {'ctx'}, use_global_device_ids=true, to_apply=%region_30.31 | all-reduce | flops 1024 | bytes 4096 | tf_op jit(solution)/shard_map/psum | solution.py:279
  914.7 196.3 %all-reduce.3.cloned.1.call-done = (bf16[256,3072]{1,0:T(8,128)(2,1)}, bf16[256,1024]{1,0:T(8,128)(2,1)}, bf16[256,4096]{1,0:T(8,128)(2,1)}, bf16[1024,1024]{1,0:T(8,128)(2,1)}) async-done(((bf16[256,3072]{1,0:T(8,128)(2,1)}, bf16[256,1024]{1,0:T(8,128)(2,1)}, bf16[256,4096]{1,0:T(8,128)(2,1)}, bf16[1024,1024]{1,0:T(8,128)(2,1)}), (bf16[256,3072]{1,0:T(8,128)(2,1)}, bf16[256,1024]{1,0:T(8,128)(2,1)}, ...) | async-done | bytes 6291472 | tf_op jit(solution)/shard_map/psum | solution.py:275
  1111.0 8.7 add_multiply_fusion.2
  1124.1 9.8 add_multiply_fusion.1
  1134.0 6.8 add_multiply_fusion
  (353 shorter events, 180.3 us)
Async XLA Ops:
  7.2 51.5 %all-gather.8.cloned.1.call-start = ((), (), s32[]{:S(2)}) async-start(), calls=%async_computation.7 | async-start | bytes 7864320 | tf_op jit(solution)/shard_map/all_gather | solution.py:83
  7.9 148.3 %all-gather.14.cloned.1.call-start = ((), (), s32[]{:S(2)}) async-start(), calls=%async_computation.16 | async-start | bytes 4718592 | tf_op jit(solution)/shard_map/all_gather | solution.py:112
  16.8 46.8 %copy-start.29 = (f32[256]{0:T(256)}, f32[256]{0:T(256)S(1)}, u32[]{:S(2)}) copy-start(f32[256]{0:T(256)S(1)} %fusion.53) | copy-start | bytes 3076
  63.6 29.7 %copy-start.34 = (s32[1,16]{1,0:T(1,128)S(1)}, s32[1,16]{1,0:T(1,128)}, u32[]{:S(2)}) copy-start(s32[1,16]{1,0:T(1,128)} %param.24) | copy-start | bytes 196
  64.8 148.0 %all-gather.16.cloned.1.call-start = ((), (), s32[]{:S(2)}) async-start(), calls=%async_computation.17 | async-start | bytes 4718592 | tf_op jit(solution)/shard_map/all_gather | solution.py:111
  65.5 228.1 %all-gather.10.cloned.1.call-start = ((), (), s32[]{:S(2)}) async-start(), calls=%async_computation.8 | async-start | bytes 2621440 | tf_op jit(solution)/shard_map/all_gather | solution.py:84
  65.6 25.6 %collective-permute-start = (bf16[1024,1024]{1,0:T(8,128)(2,1)S(1)}, bf16[1024,1024]{1,0:T(8,128)(2,1)}, u32[]{:S(2)}, u32[]{:S(2)}) collective-permute-start(bf16[1024,1024]{1,0:T(8,128)(2,1)S(1)} %copy-done.2), channel_id=1, source_target_pairs={{0,8},{8,16},{16,24},{24,0},{1,9},{9,17},{17,25},{25,1},{2,10},{10... | collective-permute-start | bytes 6291464 | tf_op jit(solution)/shard_map/ppermute | solution.py:27
  66.1 231.0 %all-gather.12.cloned.1.call-start = ((), (), s32[]{:S(2)}) async-start(), calls=%async_computation.9 | async-start | bytes 10485760 | tf_op jit(solution)/shard_map/all_gather | solution.py:85
  91.2 47.9 %collective-permute-start.1 = (bf16[1024,1024]{1,0:T(8,128)(2,1)}, bf16[1024,1024]{1,0:T(8,128)(2,1)}, u32[]{:S(2)}, u32[]{:S(2)}) collective-permute-start(bf16[1024,1024]{1,0:T(8,128)(2,1)} %collective-permute-done), channel_id=1, source_target_pairs={{0,8},{8,16},{16,24},{24,0},{1,9},{9,17},{17,25},{25,1},{2,10},{10... | collective-permute-start | bytes 6291464 | tf_op jit(solution)/shard_map/ppermute | solution.py:27
  91.2 51.6 %collective-permute-start.2 = (bf16[1024,1024]{1,0:T(8,128)(2,1)S(1)}, bf16[1024,1024]{1,0:T(8,128)(2,1)}, u32[]{:S(2)}, u32[]{:S(2)}) collective-permute-start(bf16[1024,1024]{1,0:T(8,128)(2,1)S(1)} %copy-done.2), channel_id=1, source_target_pairs={{0,24},{8,0},{16,8},{24,16},{1,25},{9,1},{17,9},{25,17},{2,26},{10... | collective-permute-start | bytes 6291464 | tf_op jit(solution)/shard_map/ppermute | solution.py:29
  92.9 438.6 %reduce-scatter.12.cloned.1.call-start = ((), (), s32[]{:S(2)}) async-start(), calls=%async_computation.11 | async-start | bytes 4718592 | tf_op jit(solution)/shard_map/reduce_scatter | solution.py:240
  150.2 5.7 copy-start.28
  219.3 75.1 %copy-start.4 = (bf16[1,256,1024]{2,1,0:T(8,128)(2,1)S(1)}, bf16[1,256,1024]{2,1,0:T(8,128)(2,1)}, u32[]{:S(2)}) copy-start(bf16[1,256,1024]{2,1,0:T(8,128)(2,1)} %param.22) | copy-start | bytes 1572868
  242.3 4.7 copy-start
  293.6 9.5 copy-start.7
  297.1 6.0 copy-start.20
  297.1 15.6 %slice-start = ((s8[8388608]{0:T(1024)(128)(4,1)}), s8[4194304]{0:T(1024)(128)(4,1)S(1)}, s32[]{:S(2)}) async-start(s8[8388608]{0:T(1024)(128)(4,1)} %bitcast.232), calls=%async_computation.20 | async-start | bytes 8388608
  303.1 9.6 copy-start.35
  303.1 9.6 slice-start.1
  317.0 7.4 copy-start.23
  331.5 4.0 copy-start.1
  346.5 4.0 copy-start.1
  376.6 4.0 copy-start.1
  444.5 179.7 %reduce-scatter.10.cloned.1.call-start = ((), (), s32[]{:S(2)}) async-start(), calls=%async_computation.10 | async-start | bytes 4718592 | tf_op jit(solution)/shard_map/reduce_scatter | solution.py:237
  445.3 213.3 %reduce-scatter.16.cloned.1.call-start = ((), (), s32[]{:S(2)}) async-start(), calls=%async_computation.13 | async-start | bytes 2621440 | tf_op jit(solution)/shard_map/reduce_scatter | solution.py:261
  448.7 284.4 %reduce-scatter.18.cloned.1.call-start = ((), (), s32[]{:S(2)}) async-start(), calls=%async_computation.14 | async-start | bytes 10485760 | tf_op jit(solution)/shard_map/reduce_scatter | solution.py:264
  456.5 350.8 %reduce-scatter.20.cloned.1.call-start = ((), (), s32[]{:S(2)}) async-start(), calls=%async_computation.15 | async-start | bytes 10485760 | tf_op jit(solution)/shard_map/reduce_scatter | solution.py:267
  466.0 158.3 %copy-start.27 = (bf16[1,256,1024]{1,2,0:T(8,128)(2,1)S(1)}, bf16[1,256,1024]{1,2,0:T(8,128)(2,1)}, u32[]{:S(2)}) copy-start(bf16[1,256,1024]{1,2,0:T(8,128)(2,1)} %get-tuple-element.320) | copy-start | bytes 1572868
  466.0 402.4 %reduce-scatter.14.cloned.1.call-start = ((), (), s32[]{:S(2)}) async-start(), calls=%async_computation.12 | async-start | bytes 7864320 | tf_op jit(solution)/shard_map/reduce_scatter | solution.py:258
  630.1 261.2 %reduce-scatter.22.cloned.1.call-start = ((), (), s32[]{:S(2)}) async-start(), calls=%async_computation.18 | async-start | bytes 327680
  630.2 5.5 copy-start.30
  638.2 472.8 %all-reduce.3.cloned.1.call-start = ((), (), s32[]{:S(2)}) async-start(), calls=%async_computation.19 | async-start | bytes 12582912 | tf_op jit(solution)/shard_map/psum | solution.py:275
  868.4 8.3 copy-start.14
  868.4 8.3 copy-start.22
  876.7 37.4 %copy-start.31 = (bf16[4,256]{1,0:T(4,128)(2,1)S(1)}, bf16[4,256]{1,0:T(4,128)(2,1)}, u32[]{:S(2)}) copy-start(bf16[4,256]{1,0:T(4,128)(2,1)} %param.29) | copy-start | bytes 6148
  876.7 37.4 %copy-start.32 = (f32[4,256]{1,0:T(4,128)S(1)}, f32[4,256]{1,0:T(4,128)}, u32[]{:S(2)}) copy-start(f32[4,256]{1,0:T(4,128)} %param.34) | copy-start | bytes 12292
  876.7 37.4 %copy-start.33 = (f32[4,256]{1,0:T(4,128)S(1)}, f32[4,256]{1,0:T(4,128)}, u32[]{:S(2)}) copy-start(f32[4,256]{1,0:T(4,128)} %param.39) | copy-start | bytes 12292
  876.7 234.3 %copy-start.6 = (bf16[256,3072]{1,0:T(8,128)(2,1)S(1)}, bf16[256,3072]{1,0:T(8,128)(2,1)}, u32[]{:S(2)}) copy-start(bf16[256,3072]{1,0:T(8,128)(2,1)} %param.25) | copy-start | bytes 4718596
  1111.0 8.7 copy-start.17
  1111.0 8.7 copy-start.24
  1111.0 8.7 copy-start.25
  1111.0 8.7 copy-start.26
  1111.0 11.2 copy-start.10
  1119.7 4.4 copy-start.9
  1124.1 9.9 copy-start.3
  1124.1 9.9 copy-start.11
  1124.1 9.9 copy-start.12
  1124.1 9.9 copy-start.16
  (20 other events, 57.3 us)
Sparse Core Ops, SparseCore 0:
  9.6 49.0 all-gather.7
  64.9 73.4 all-gather.13
  141.1 71.6 all-gather.15
  214.2 20.8 all-gather.9
  236.5 58.2 all-gather.11
  444.7 86.7 reduce-scatter.11
  536.1 88.0 reduce-scatter.9
  627.4 31.1 reduce-scatter.15
  661.3 71.7 reduce-scatter.17
  735.5 71.7 reduce-scatter.19
  810.0 58.3 reduce-scatter.13
  871.3 20.0 reduce-scatter.21
  896.4 214.5 all-reduce.2
